TPU v7x, 256 devices: a whole 4x4x8 slice. The times are simulated.
256 devices in a mesh: dp: 8 (over x_hi, y), fsdp: 16 (over z, core), tensor: 2 (over x_lo).
Axes of the slice: x: 4 (x_hi: 2, x_lo: 2; x = x_hi * 2 + x_lo), y: 4, z: 8, core: 2. Of those that a mesh axis runs over, the one named last changes fastest.
Arguments:
- attn_out: bfloat16 [16384, 2560], P(('dp', 'fsdp')), may hold values from -6 to 6
- cotangent: bfloat16 [16384, 5120], P(('dp', 'fsdp'), 'tensor'), may hold values from -6 to 6
- old_weights: bfloat16 [3, 2048, 4096], P(None, 'tensor', 'fsdp'), may hold values from -0.125 to 0.125
- depth_coef: float32 [2], replicated, may hold values from 0.3 to 1
- depth_pick: int32 [2], replicated, may hold values from 0 to 2
- in_blocks: bfloat16 [20, 2, 128, 128], replicated, may hold values from -0.3125 to 0.3125
- in_cols: int32 [20, 2], replicated, may hold values from 0 to 15, all different within a row
- out_blocks: bfloat16 [40, 2, 128, 128], P('tensor'), may hold values from -0.375 to 0.375
- out_cols: int32 [40, 2], P('tensor'), may hold values from 0 to 31, all different within a row
Outputs:
- grown_out: bfloat16 [16384, 5120], P(('dp', 'fsdp'), 'tensor')
- grad_attn: bfloat16 [16384, 2560], P(('dp', 'fsdp'), 'tensor')
- grad_in_blocks: float32 [20, 2, 128, 128], P('tensor')
- grad_out_blocks: float32 [40, 2, 128, 128], P('tensor')
Inputs may be any that keep to these rules, and one draw needn't show every extreme that they name: `in_cols`: each row names 2 different old head blocks; every old head block is named by some row. `out_cols`: each row names 2 different old width blocks; every old width block is named by some row.
All inputs are finite; a program needn't handle non-finite values.
Results may differ from a plain program's by a relative error of at most 0.0095.
Values may be sent and summed in bfloat16 or wider, within the bound.
No kernel may reach another device: no remote copies, remote signals or barrier semaphores. Data moves between devices by JAX's collectives and lax.ppermute only.
A program may use at most 64 MiB of HBM per device.

v0:
```python
import jax
import jax.numpy as jnp
from jax import lax
from jax.sharding import PartitionSpec as P

HEAD = 128
D_OLD = 4096
HG_OLD = 16
HG_NEW = 20
DEPTH_K = 2
BO_OLD = 32


def gathered_mix(mixed_weight):
    return lax.all_gather(mixed_weight, "fsdp", axis=1, tiled=True)


def local(
    attn_out,
    cotangent,
    old_weights,
    depth_coef,
    depth_pick,
    in_blocks,
    in_cols,
    out_blocks,
    out_cols,
):
    highest = lax.Precision.HIGHEST
    tok_rows = attn_out.shape[0]
    tensor_half = lax.axis_index("tensor")
    tensor_count = lax.axis_size("tensor")
    local_old = old_weights.shape[1]
    local_blocks = local_old // HEAD
    rows_in = HG_NEW // tensor_count
    mixed_weight = jnp.zeros(old_weights.shape[1:], jnp.float32)
    for layer_slot in range(DEPTH_K):
        picked = lax.dynamic_index_in_dim(old_weights, depth_pick[layer_slot], 0, keepdims=False)
        mixed_weight = mixed_weight + depth_coef[layer_slot] * picked.astype(jnp.float32)
    mixed_weight = mixed_weight.astype(jnp.bfloat16)
    attn_blocks = attn_out.reshape(tok_rows, HG_NEW, HEAD)
    products = jnp.einsum(
        "trd,rkde->trke", attn_blocks, in_blocks, preferred_element_type=jnp.float32
    )
    local_cols = tensor_half * local_blocks + jnp.arange(local_blocks, dtype=jnp.int32)
    in_hot = (in_cols[:, :, None] == local_cols[None, None, :]).astype(jnp.float32)
    hidden_local = jnp.einsum("trke,rkc->tce", products, in_hot, precision=highest)
    hidden_local = hidden_local.reshape(tok_rows, local_old).astype(jnp.bfloat16)
    full_mix = gathered_mix(mixed_weight)
    old_part = jnp.dot(hidden_local, full_mix, preferred_element_type=jnp.float32)
    old_out = lax.psum(old_part.astype(jnp.bfloat16), "tensor")
    old_selected = jnp.take(old_out.reshape(tok_rows, BO_OLD, HEAD), out_cols, axis=1)
    grown_out = jnp.einsum(
        "trkd,rkde->tre", old_selected, out_blocks, preferred_element_type=jnp.float32
    )
    grown_out = grown_out.reshape(tok_rows, -1).astype(jnp.bfloat16)
    cot_blocks = cotangent.reshape(tok_rows, out_blocks.shape[0], HEAD)
    backward_terms = jnp.einsum(
        "tre,rkde->trkd", cot_blocks, out_blocks, preferred_element_type=jnp.float32
    )
    out_hot = (out_cols[:, :, None] == jnp.arange(BO_OLD, dtype=jnp.int32)[None, None, :]).astype(
        jnp.float32
    )
    grad_part = jnp.einsum("trkd,rkc->tcd", backward_terms, out_hot, precision=highest).reshape(
        tok_rows, D_OLD
    )
    old_grad = lax.psum(grad_part.astype(jnp.bfloat16), "tensor")
    hidden_grad_local = jnp.einsum(
        "to,fo->tf", old_grad, full_mix, preferred_element_type=jnp.float32
    ).astype(jnp.bfloat16)
    hidden_grad = lax.all_gather(hidden_grad_local, "tensor", axis=1, tiled=True)
    my_in_blocks = lax.dynamic_slice_in_dim(in_blocks, tensor_half * rows_in, rows_in, 0)
    my_in_cols = lax.dynamic_slice_in_dim(in_cols, tensor_half * rows_in, rows_in, 0)
    grad_selected = jnp.take(hidden_grad.reshape(tok_rows, HG_OLD, HEAD), my_in_cols, axis=1)
    grad_attn = jnp.einsum(
        "trke,rkde->trd", grad_selected, my_in_blocks, preferred_element_type=jnp.float32
    )
    grad_attn = grad_attn.reshape(tok_rows, rows_in * HEAD).astype(jnp.bfloat16)
    my_attn = lax.dynamic_slice_in_dim(attn_blocks, tensor_half * rows_in, rows_in, 1)
    in_terms = jnp.einsum(
        "trd,trke->rkde", my_attn, grad_selected, preferred_element_type=jnp.float32
    )
    out_terms = jnp.einsum(
        "trkd,tre->rkde", old_selected, cot_blocks, preferred_element_type=jnp.float32
    )
    in_sum, out_sum = lax.psum((in_terms, out_terms), ("dp", "fsdp"))
    grad_scale = float(tok_rows * lax.axis_size("dp") * lax.axis_size("fsdp")) ** (-0.5)
    return (grown_out, grad_attn, in_sum * grad_scale, out_sum * grad_scale)


def solution(mesh):
    placed = (
        P(("dp", "fsdp"), None),
        P(("dp", "fsdp"), "tensor"),
        P(None, "tensor", "fsdp"),
        P(),
        P(),
        P(),
        P(),
        P("tensor", None, None, None),
        P("tensor", None),
    )
    return jax.shard_map(
        local,
        mesh=mesh,
        in_specs=placed,
        out_specs=(
            P(("dp", "fsdp"), "tensor"),
            P(("dp", "fsdp"), "tensor"),
            P("tensor", None, None, None),
            P("tensor", None, None, None),
        ),
        check_vma=False,
    )
```

profile of v0, /device:TPU:6, one launch (start us, length us, event | category | flops | bytes accessed | tf_op | source)
XLA Modules:
  0.0 1481.5 jit_solution(9573268355496351866)
XLA Ops:
  7.2 0.0 copy-start
  7.2 0.0 all-gather.3.cloned.1.call-start
  7.2 1.3 fusion.55
  11.2 1.3 fusion.54
  13.8 3.5 add_convert_fusion
  17.3 0.0 copy-start.6
  17.3 0.0 all-gather.3.cloned.1.call-update
  17.4 0.0 all-reduce.7.cloned.1.call-start
  17.4 1.5 copy.27
  18.9 0.0 copy-start.1
  18.9 0.0 copy-done.6
  18.9 2.0 fusion.56
  21.0 0.0 copy-done.1
  21.0 0.0 copy-start.7
  21.0 3.6 copy.45
  24.6 0.0 copy-done.7
  24.6 0.3 copy.34
  24.9 0.0 copy-done
  24.9 2.0 fusion.57
  26.9 3.6 copy.51
  30.5 0.0 copy-done.9
  30.5 3.5 bitcast_convert_fusion
  34.0 0.0 copy-start.8
  34.0 1.4 copy.71
  35.5 0.0 copy-done.8
  35.5 3.0 fusion.24
  38.5 46.0 %all-gather.3.cloned.1.call-done = bf16[1,1024,4096]{2,1,0:T(8,128)(2,1)} async-done(((bf16[1,1024,256]{2,1,0:T(8,128)(2,1)}), bf16[1,1024,4096]{2,1,0:T(8,128)(2,1)}) %all-gather.3.cloned.1.call-update) | async-done | bytes 8388624 | tf_op jit(solution)/shard_map/all_gather | solution.py:15
  84.5 4.7 fusion.13
  89.1 1.3 copy.72
  90.4 0.0 all-reduce.7.cloned.1.call-update
  90.4 0.0 all-reduce.5.cloned.1.call-start
  90.5 0.1 compare_and_fusion
  90.6 0.1 copy.35
  90.7 0.1 reshape.66
  90.7 0.1 copy.33
  90.8 0.1 copy.29
  91.0 0.1 reshape.58
  91.1 0.1 copy.26
  91.2 72.4 %all-reduce.7.cloned.1.call-done = (bf16[128,32,128]{2,0,1:T(8,128)(2,1)}, bf16[128,4096]{1,0:T(8,128)(2,1)}) async-done(((bf16[128,32,128]{2,0,1:T(8,128)(2,1)}, bf16[128,4096]{1,0:T(8,128)(2,1)}), (bf16[128,32,128]{2,0,1:T(8,128)(2,1)}, bf16[128,4096]{1,0:T(8,128)(2,1)})) %all-reduce.7.cloned.1.call-update) | async-done | bytes 2097168 | tf_op jit(solution)/shard_map/psum | solution.py:51
  163.5 6.6 fusion.27
  170.2 8.7 all_gather.7
  178.9 0.1 copy_bitcast_fusion.2
  179.0 0.7 gather_fusion.1
  179.7 1.1 copy.37
  180.8 3.1 gather_fusion
  183.9 1.8 copy.30
  185.6 0.0 copy-start.2
  185.6 0.0 copy-start.3
  185.7 2.0 fusion.17
  187.7 0.0 copy-done.2
  187.7 0.0 copy-done.3
  187.7 1.4 convolution_bitcast_fusion
  189.1 0.0 copy-start.4
  189.1 0.0 all-reduce.5.cloned.1.call-update
  189.2 1.1 copy-done.4
  190.2 2.2 fusion.23
  192.4 1.9 copy.42
  194.3 0.6 fusion.16
  194.9 1.1 copy.41
  196.0 1273.8 %all-reduce.5.cloned.1.call-done = (f32[10,2,128,128]{2,3,1,0:T(8,128)}, f32[20,2,128,128]{3,2,1,0:T(8,128)}) async-done(((f32[10,2,128,128]{2,3,1,0:T(8,128)}, f32[20,2,128,128]{3,2,1,0:T(8,128)}), (f32[10,2,128,128]{2,3,1,0:T(8,128)}, f32[20,2,128,128]{3,2,1,0:T(8,128)})) %all-reduce.5.cloned.1.call-update) | async-done | bytes 3932176 | tf_op jit(solution)/shard_map/psum | solution.py:86
  1469.8 3.6 broadcast_multiply_fusion
  1473.4 0.0 copy-done.5
  1473.4 0.1 broadcast_multiply_fusion.1
  1473.5 1.5 copy.43
  (7 shorter events, 0.0 us)
Async XLA Ops:
  7.2 17.8 %copy-start = (bf16[20,2,128,128]{3,2,1,0:T(8,128)(2,1)S(1)}, bf16[20,2,128,128]{3,2,1,0:T(8,128)(2,1)}, u32[]{:S(2)}) copy-start(bf16[20,2,128,128]{3,2,1,0:T(8,128)(2,1)} %param.16) | copy-start | bytes 3932164
  7.2 77.3 %all-gather.3.cloned.1.call-start = ((), (), s32[]{:S(2)}) async-start(), calls=%async_computation | async-start | bytes 8912896 | tf_op jit(solution)/shard_map/all_gather | solution.py:15
  17.3 1.6 copy-start.6
  17.4 146.2 %all-reduce.7.cloned.1.call-start = ((), (), s32[]{:S(2)}) async-start(), calls=%async_computation.2 | async-start | bytes 4194304 | tf_op jit(solution)/shard_map/psum | solution.py:51
  18.9 2.1 copy-start.1
  21.0 3.6 copy-start.7
  26.9 3.6 copy-start.9
  34.0 1.4 copy-start.8
  90.4 1379.4 %all-reduce.5.cloned.1.call-start = ((), (), s32[]{:S(2)}) async-start(), calls=%async_computation.1 | async-start | bytes 7864320 | tf_op jit(solution)/shard_map/psum | solution.py:86
  185.6 2.1 copy-start.2
  185.6 2.1 copy-start.3
  189.1 1.1 copy-start.4
  1469.8 3.6 copy-start.5
Sparse Core Ops, SparseCore 0:
  17.5 66.9 all-gather.2
  90.5 72.9 all-reduce.6
  189.3 1280.4 all-reduce.4
where the time goes:
time: 1480 us
  waiting for transfers between devices  1390 us (94%)
  matrix products  28.2 us (2%)
  local copies, waits for them, and re-layouts  27.2 us (2%)
  between operations  17.8 us (1%)
    psum x1, waiting for transfers between devices, local(): in_sum, out_sum = lax.psum((in_terms, out_terms), ('dp', 'fsdp'))  1270 us
    psum x1, waiting for transfers between devices, local(): old_out = lax.psum(old_part.astype(jnp.bfloat16), 'tensor')  72.4 us
    all_gather x1, waiting for transfers between devices, gathered_mix(): return lax.all_gather(mixed_weight, 'fsdp', axis=1, tiled=True)  46 us
  transfers between devices with their start and end apart: 3, of which 3 were waited for; matrix products, arithmetic and copies ran while one was open for 2% of the time, Pallas kernels for 0%

commit v1 on v0

--- a/solution.py
+++ b/solution.py
@@ -83,7 +83,7 @@
     out_terms = jnp.einsum(
         "trkd,tre->rkde", old_selected, cot_blocks, preferred_element_type=jnp.float32
     )
-    in_sum, out_sum = lax.psum((in_terms, out_terms), ("dp", "fsdp"))
+    in_sum, out_sum = lax.psum(lax.psum((in_terms, out_terms), "dp"), "fsdp")
     grad_scale = float(tok_rows * lax.axis_size("dp") * lax.axis_size("fsdp")) ** (-0.5)
     return (grown_out, grad_attn, in_sum * grad_scale, out_sum * grad_scale)
 

time: 1480 us -> 438 us (0.30)
  waiting for transfers between devices: 1390 us -> 348 us
    psum x1 -> x2, waiting for transfers between devices: 1270 us -> 229 us  [local(): in_sum, out_sum = lax.psum(lax.psum((in_terms, out_terms), 'dp'), 'fsdp')]
  transfers between devices with their start and end apart: 3 -> 4, of which waited for: 3 -> 4; matrix products, arithmetic and copies ran while one was open for 2% -> 6% of each run, Pallas kernels for 0% -> 0%
where the time goes in v1:
time: 438 us; the launch traced here: 437 us
  waiting for transfers between devices  348 us (79%)
  matrix products  28.2 us (6%)
  local copies, waits for them, and re-layouts  27.1 us (6%)
  between operations  17.8 us (4%)
  blocking collectives  8.54 us (2%)
  other arithmetic  7.38 us (2%)
    psum x2, waiting for transfers between devices, local(): in_sum, out_sum = lax.psum(lax.psum((in_terms, out_terms), 'dp'), 'fsdp')  229 us
    psum x1, waiting for transfers between devices, local(): old_out = lax.psum(old_part.astype(jnp.bfloat16), 'tensor')  72.7 us
    all_gather x1, waiting for transfers between devices, gathered_mix(): return lax.all_gather(mixed_weight, 'fsdp', axis=1, tiled=True)  46 us
  transfers between devices with their start and end apart: 4, of which 4 were waited for; matrix products, arithmetic and copies ran while one was open for 6% of the time, Pallas kernels for 0%

profile of v1, /device:TPU:6, one launch (start us, length us, event | category | flops | bytes accessed | tf_op | source)
XLA Modules:
  0.0 437.3 jit_solution(12904491024456688300)
XLA Ops:
  7.2 0.0 copy-start
  7.2 0.0 all-gather.3.cloned.1.call-start
  7.2 1.3 fusion.55
  11.2 1.3 fusion.54
  13.8 3.5 add_convert_fusion
  17.3 0.0 all-gather.3.cloned.1.call-update
  17.4 0.0 all-reduce.11.cloned.1.call-start
  17.4 1.5 copy.27
  18.9 0.0 copy-start.1
  18.9 0.0 copy-done.6
  18.9 2.0 fusion.56
  21.0 0.0 copy-done.1
  21.0 3.6 copy.45
  24.6 0.0 copy-done.7
  24.6 0.3 copy.34
  24.9 0.0 copy-done
  24.9 2.0 fusion.57
  26.9 3.6 copy.51
  30.4 0.0 copy-done.9
  30.4 3.5 bitcast_convert_fusion
  34.0 0.0 copy-start.8
  34.0 1.4 copy.71
  35.4 0.0 copy-done.8
  35.4 3.0 fusion.24
  38.4 46.0 %all-gather.3.cloned.1.call-done = bf16[1,1024,4096]{2,1,0:T(8,128)(2,1)} async-done(((bf16[1,1024,256]{2,1,0:T(8,128)(2,1)}), bf16[1,1024,4096]{2,1,0:T(8,128)(2,1)}) %all-gather.3.cloned.1.call-update) | async-done | bytes 8388624 | tf_op jit(solution)/shard_map/all_gather | solution.py:15
  84.4 4.7 %fusion.13 = bf16[16,32,8,128]{3,2,1,0:T(8,128)(2,1)S(1)} fusion(bf16[1,1024,4096]{2,1,0:T(8,128)(2,1)} %all-gather.3.cloned.1.call-done, bf16[16,8,8,128]{3,2,1,0:T(8,128)(2,1)S(1)} %bitcast.126), kind=kOutput, calls=%fused_computation.14 | convolution fusion | flops 1074266112 | bytes 9699328 | tf_op jit(solution)/shard_map/dot_general | solution.py:50
  89.1 1.3 copy.72
  90.4 0.0 all-reduce.11.cloned.1.call-update
  90.4 0.0 all-reduce.9.cloned.1.call-start
  90.4 0.1 compare_and_fusion
  90.5 0.1 copy.35
  90.6 0.1 reshape.66
  90.7 0.1 copy.33
  90.8 0.1 copy.29
  90.9 0.1 reshape.58
  91.0 0.1 copy.26
  91.2 72.7 %all-reduce.11.cloned.1.call-done = (bf16[128,32,128]{2,0,1:T(8,128)(2,1)}, bf16[128,4096]{1,0:T(8,128)(2,1)}) async-done(((bf16[128,32,128]{2,0,1:T(8,128)(2,1)}, bf16[128,4096]{1,0:T(8,128)(2,1)}), (bf16[128,32,128]{2,0,1:T(8,128)(2,1)}, bf16[128,4096]{1,0:T(8,128)(2,1)})) %all-reduce.11.cloned.1.call-update) | async-done | bytes 2097168 | tf_op jit(solution)/shard_map/psum | solution.py:51
  163.9 6.6 %fusion.27 = bf16[128,1024]{1,0:T(8,128)(2,1)S(1)} fusion(bf16[128,4096]{1,0:T(8,128)(2,1)} %get-tuple-element.17, bf16[1,1024,4096]{2,1,0:T(8,128)(2,1)} %all-gather.3.cloned.1.call-done), kind=kOutput, calls=%fused_computation.25 | convolution fusion | flops 1073872896 | bytes 9699328 | tf_op jit(solution)/shard_map/to,fo->tf/dot_general | solution.py:68
  170.5 8.5 %all_gather.7 = bf16[128,2048]{1,0:T(8,128)(2,1)S(1)} all-gather(bf16[128,1024]{1,0:T(8,128)(2,1)S(1)} %fusion.27), channel_id=1, replica_groups=mesh['dp'=8,'fsdp'=16,'tensor'=2] {'tensor'}, dimensions={1}, use_global_device_ids=true | all-gather | bytes 786432 | tf_op jit(solution)/shard_map/all_gather | solution.py:71
  179.1 0.1 copy_bitcast_fusion.2
  179.2 0.7 gather_fusion.1
  179.9 1.1 copy.37
  181.0 3.1 gather_fusion
  184.0 1.8 copy.30
  185.8 0.0 copy-start.2
  185.8 0.0 copy-start.3
  185.8 2.0 fusion.17
  187.9 0.0 copy-done.2
  187.9 0.0 copy-done.3
  187.9 1.4 convolution_bitcast_fusion
  189.3 0.0 all-reduce.9.cloned.1.call-update
  189.3 0.0 all-reduce.7.cloned.1.call-start
  189.4 111.8 %all-reduce.9.cloned.1.call-done = (f32[10,2,128,128]{2,3,1,0:T(8,128)}, f32[20,2,128,128]{3,2,1,0:T(8,128)}) async-done(((f32[10,2,128,128]{2,3,1,0:T(8,128)}, f32[20,2,128,128]{3,2,1,0:T(8,128)}), (f32[10,2,128,128]{2,3,1,0:T(8,128)}, f32[20,2,128,128]{3,2,1,0:T(8,128)})) %all-reduce.9.cloned.1.call-update) | async-done | bytes 3932176 | tf_op jit(solution)/shard_map/psum | solution.py:86
  301.2 0.0 all-reduce.7.cloned.1.call-update
  301.2 1.1 copy-done.4
  302.2 2.2 fusion.23
  304.4 1.9 copy.42
  306.3 0.6 fusion.16
  306.9 1.1 copy.41
  308.0 117.5 %all-reduce.7.cloned.1.call-done = (f32[10,2,128,128]{2,3,1,0:T(8,128)}, f32[20,2,128,128]{3,2,1,0:T(8,128)}) async-done(((f32[10,2,128,128]{2,3,1,0:T(8,128)}, f32[20,2,128,128]{3,2,1,0:T(8,128)}), (f32[10,2,128,128]{2,3,1,0:T(8,128)}, f32[20,2,128,128]{3,2,1,0:T(8,128)})) %all-reduce.7.cloned.1.call-update) | async-done | bytes 3932176 | tf_op jit(solution)/shard_map/psum | solution.py:86
  425.6 3.6 broadcast_multiply_fusion
  429.2 0.0 copy-done.5
  429.2 0.1 broadcast_multiply_fusion.1
  429.3 1.5 copy.43
  (10 shorter events, 0.0 us)
Async XLA Ops:
  7.2 17.7 %copy-start = (bf16[20,2,128,128]{3,2,1,0:T(8,128)(2,1)S(1)}, bf16[20,2,128,128]{3,2,1,0:T(8,128)(2,1)}, u32[]{:S(2)}) copy-start(bf16[20,2,128,128]{3,2,1,0:T(8,128)(2,1)} %param.16) | copy-start | bytes 3932164
  7.2 77.2 %all-gather.3.cloned.1.call-start = ((), (), s32[]{:S(2)}) async-start(), calls=%async_computation | async-start | bytes 8912896 | tf_op jit(solution)/shard_map/all_gather | solution.py:15
  17.3 1.6 copy-start.6
  17.4 146.5 %all-reduce.11.cloned.1.call-start = ((), (), s32[]{:S(2)}) async-start(), calls=%async_computation.3 | async-start | bytes 4194304 | tf_op jit(solution)/shard_map/psum | solution.py:51
  18.9 2.1 copy-start.1
  21.0 3.6 copy-start.7
  26.9 3.6 copy-start.9
  34.0 1.4 copy-start.8
  90.4 210.8 %all-reduce.9.cloned.1.call-start = ((), (), s32[]{:S(2)}) async-start(), calls=%async_computation.2 | async-start | bytes 7864320 | tf_op jit(solution)/shard_map/psum | solution.py:86
  185.8 2.1 copy-start.2
  185.8 2.1 copy-start.3
  189.3 236.2 %all-reduce.7.cloned.1.call-start = ((), (), s32[]{:S(2)}) async-start(), calls=%async_computation.1 | async-start | bytes 7864320 | tf_op jit(solution)/shard_map/psum | solution.py:86
  301.2 1.1 copy-start.4
  425.6 3.6 copy-start.5
Sparse Core Ops, SparseCore 0:
  17.5 66.9 all-gather.2
  90.5 73.3 all-reduce.10
  189.5 111.6 all-reduce.8
  303.5 122.0 all-reduce.6
